TPU v7x, 128 devices: a whole 4x4x4 slice. The times are simulated.
128 devices in a mesh: lon: 8 (over z, y_hi), lat: 16 (over y_lo, x, core).
Axes of the slice: x: 4, y: 4 (y_hi: 2, y_lo: 2; y = y_hi * 2 + y_lo), z: 4, core: 2. Of those that a mesh axis runs over, the one named last changes fastest.
Arguments:
- atmos_state: bfloat16 [512, 512, 256], P('lat', 'lon'), may hold values from -6 to 6
- atmos_weights: bfloat16 [9, 256, 256], replicated, may hold values from -0.125 to 0.125
- flux_project: bfloat16 [256, 64], replicated, may hold values from -0.75 to 0.75
- source_row: int32 [512, 512, 4], P('lat', 'lon'), may hold values from 0 to 511, as said below
- source_col: int32 [512, 512, 4], P('lat', 'lon'), may hold values from 0 to 511, as said below
- intersection_weight: float32 [512, 512, 4], P('lat', 'lon'), may hold values from 0 to 1
- ocean_state: bfloat16 [512, 512, 256], P('lat', 'lon'), may hold values from -6 to 6
- flux_inject: bfloat16 [64, 256], replicated, may hold values from -0.75 to 0.75
- ocean_mask: int32 [512, 512], P('lat', 'lon'), may hold values 0 or 1
- ocean_weights: bfloat16 [9, 256, 256], replicated, may hold values from -0.125 to 0.125
- out_cotangent: bfloat16 [512, 512, 256], P('lat', 'lon'), may hold values from -6 to 6
Outputs:
- ocean_out: bfloat16 [512, 512, 256], P('lat', 'lon')
- grad_atmos: float32 [9, 256, 256], replicated
- grad_ocean: float32 [9, 256, 256], replicated
- grad_project: float32 [256, 64], replicated
- grad_inject: float32 [64, 256], replicated
Inputs may be any that keep to these rules, and one draw needn't show every extreme that they name: `source_row`: entry k of ocean cell (j, i) names an atmosphere row within 2 rows of j; for ocean rows j >= 512 - 32 (the band beside the fold) within 32 rows of j; both reaches are attained. `source_col`: entry k of ocean cell (j, i) names an atmosphere column within 2 columns of i, counted cyclically; for ocean rows j >= 480 within 64 columns of i; both reaches are attained.
All inputs are finite; a program needn't handle non-finite values. No bound on the sum of `ocean_mask` on one device may be relied on, other than what follows from the above.
Results may differ from a plain program's by a relative error of at most 0.018.
Values may be sent and summed in bfloat16 or wider, within the bound.
No kernel may reach another device: no remote copies, remote signals or barrier semaphores. Data moves between devices by JAX's collectives and lax.ppermute only.
A program may use at most 128 MiB of HBM per device.

v0:
```python
import jax
import jax.numpy as jnp
from jax import lax
from jax.sharding import PartitionSpec as P


def passed_along(x, axis, by):
    length = lax.axis_size(axis)
    pairs = [(i, i + by) for i in range(length) if 0 <= i + by < length]
    return lax.ppermute(x, axis, pairs)


def shifted(x, axis, by):
    length = lax.axis_size(axis)
    return lax.ppermute(x, axis, [(i, (i + by) % length) for i in range(length)])


def partner(x, axis, distance):
    return lax.ppermute(x, axis, [(i, i ^ 1 << distance) for i in range(lax.axis_size(axis))])


def lat_move(field, offset):
    return passed_along(field, "lat", offset)


def lon_move(field, offset):
    return shifted(field, "lon", offset)


def mirror_row(edge_row):
    moved = edge_row
    for bit_number in range(lax.axis_size("lon").bit_length() - 1):
        moved = partner(moved, "lon", bit_number)
    return moved[:, ::-1]


def pad_field(field, is_top, folding):
    south = lat_move(field[-1:], 1)
    north = lat_move(field[:1], -1)
    if folding:
        north = jnp.where(is_top, mirror_row(field[-1:]), north)
    padded = jnp.concatenate([south, field, north], 0)
    west = lon_move(padded[:, -1:], 1)
    east = lon_move(padded[:, :1], -1)
    return jnp.concatenate([west, padded, east], 1)


def silu_slope(value):
    sigma = jax.nn.sigmoid(value)
    return sigma * (1.0 + value * (1.0 - sigma))


def convolve(padded, weights, row_count, col_count):
    total = jnp.zeros((row_count * col_count, weights.shape[2]), jnp.float32)
    for tap_index in range(9):
        row_off, col_off = divmod(tap_index, 3)
        window = padded[row_off : row_off + row_count, col_off : col_off + col_count].reshape(
            row_count * col_count, -1
        )
        total = total + jnp.dot(window, weights[tap_index], preferred_element_type=jnp.float32)
    return total


def kernel_grads(padded, delta, row_count, col_count):
    result = []
    for tap_index in range(9):
        row_off, col_off = divmod(tap_index, 3)
        window = padded[row_off : row_off + row_count, col_off : col_off + col_count].reshape(
            row_count * col_count, -1
        )
        result.append(jnp.einsum("nc,nd->cd", window, delta, preferred_element_type=jnp.float32))
    return jnp.stack(result)


def transpose_conv(delta_pad, weights, is_top, row_count, col_count):
    dims = (((1,), (1,)), ((), ()))
    north = delta_pad[-1:]
    plain = jnp.concatenate([delta_pad[:-1], jnp.where(is_top, jnp.zeros_like(north), north)], 0)
    total = jnp.zeros((row_count * col_count, weights.shape[1]), jnp.float32)
    for tap_index in range(9):
        row_off, col_off = divmod(tap_index, 3)
        window = plain[
            2 - row_off : 2 - row_off + row_count, 2 - col_off : 2 - col_off + col_count
        ].reshape(row_count * col_count, -1)
        total = total + lax.dot_general(
            window, weights[tap_index], dims, preferred_element_type=jnp.float32
        )
    total = total.reshape(row_count, col_count, -1)
    seam_term = jnp.zeros((col_count, weights.shape[1]), jnp.float32)
    for col_off in range(3):
        seam_term = seam_term + lax.dot_general(
            north[0, col_off : col_off + col_count],
            weights[6 + col_off],
            dims,
            preferred_element_type=jnp.float32,
        )
    seam_term = jnp.where(is_top, seam_term, jnp.zeros_like(seam_term))
    return total.at[row_count - 1].add(seam_term)


def body(
    atmos_state,
    atmos_weights,
    flux_project,
    source_row,
    source_col,
    intersection_weight,
    ocean_state,
    flux_inject,
    ocean_mask,
    ocean_weights,
    out_cotangent,
):
    row_count, col_count, chans = atmos_state.shape
    flux_chans = flux_project.shape[1]
    cells = row_count * col_count
    dims = (((1,), (1,)), ((), ()))
    lat_here = lax.axis_index("lat")
    lon_here = lax.axis_index("lon")
    lon_count = lax.axis_size("lon")
    is_top = lat_here == lax.axis_size("lat") - 1
    land = ocean_mask.astype(jnp.float32)[..., None]
    atmos_padded = pad_field(atmos_state, is_top, False)
    atmos_pre = convolve(atmos_padded, atmos_weights, row_count, col_count)
    atmos_act = jax.nn.silu(atmos_pre).astype(jnp.bfloat16)
    flux = jnp.dot(atmos_act, flux_project, preferred_element_type=jnp.float32).astype(jnp.bfloat16)
    flux_flat = flux.reshape(row_count, col_count * flux_chans)
    band = jnp.stack([lon_move(flux_flat, 1), flux_flat, lon_move(flux_flat, -1)])
    neighbourhood = jnp.stack([lat_move(band, 1), band, lat_move(band, -1)]).reshape(
        9 * cells, flux_chans
    )
    tile_dr = source_row // row_count - lat_here
    tile_dc = jnp.remainder(source_col // col_count - lon_here + 1, lon_count) - 1
    slots = (
        ((tile_dr + 1) * 3 + tile_dc + 1) * cells
        + jnp.remainder(source_row, row_count) * col_count
        + jnp.remainder(source_col, col_count)
    )
    picked = jnp.take(neighbourhood, slots, axis=0).astype(jnp.float32)
    remapped = (
        jnp.sum(intersection_weight[..., None] * picked, axis=2)
        .astype(jnp.bfloat16)
        .reshape(cells, flux_chans)
    )
    injected = jnp.dot(remapped, flux_inject, preferred_element_type=jnp.float32).reshape(
        row_count, col_count, chans
    )
    mixed = (land * (ocean_state.astype(jnp.float32) + injected)).astype(jnp.bfloat16)
    ocean_padded = pad_field(mixed, is_top, True)
    ocean_pre = convolve(ocean_padded, ocean_weights, row_count, col_count).reshape(
        row_count, col_count, chans
    )
    ocean_out = (land * jax.nn.silu(ocean_pre)).astype(jnp.bfloat16)
    ocean_delta = (out_cotangent.astype(jnp.float32) * land * silu_slope(ocean_pre)).astype(
        jnp.bfloat16
    )
    grad_ocean = kernel_grads(ocean_padded, ocean_delta.reshape(cells, chans), row_count, col_count)
    delta_padded = pad_field(ocean_delta, is_top, True)
    ocean_back = transpose_conv(delta_padded, ocean_weights, is_top, row_count, col_count)
    mixed_grad = (land * ocean_back).astype(jnp.bfloat16).reshape(cells, chans)
    grad_inject = jnp.einsum("nf,nc->fc", remapped, mixed_grad, preferred_element_type=jnp.float32)
    remap_grad = lax.dot_general(
        mixed_grad, flux_inject, dims, preferred_element_type=jnp.float32
    ).astype(jnp.bfloat16)
    remap_grad = remap_grad.reshape(row_count, col_count, flux_chans)
    contrib_all = intersection_weight[..., None] * remap_grad.astype(jnp.float32)[:, :, None, :]
    credit = (
        jnp.zeros((9 * cells, flux_chans), jnp.float32)
        .at[slots.reshape(-1)]
        .add(contrib_all.reshape(-1, flux_chans))
    )
    credit = credit.astype(jnp.bfloat16).reshape(3, 3, row_count, col_count * flux_chans)
    routed = jnp.stack([lat_move(credit[2], 1), credit[1], lat_move(credit[0], -1)])
    from_east = lon_move(routed[:, 0], -1)
    from_west = lon_move(routed[:, 2], 1)
    flux_sum = (
        jnp.sum(routed[:, 1].astype(jnp.float32), 0)
        + jnp.sum(from_east.astype(jnp.float32), 0)
        + jnp.sum(from_west.astype(jnp.float32), 0)
    )
    flux_grad = flux_sum.astype(jnp.bfloat16).reshape(cells, flux_chans)
    grad_project = jnp.einsum("nc,nf->cf", atmos_act, flux_grad, preferred_element_type=jnp.float32)
    act_grad = lax.dot_general(flux_grad, flux_project, dims, preferred_element_type=jnp.float32)
    atmos_delta = (act_grad * silu_slope(atmos_pre)).astype(jnp.bfloat16)
    grad_atmos = kernel_grads(atmos_padded, atmos_delta, row_count, col_count)
    grad_atmos, grad_ocean, grad_project, grad_inject = lax.psum(
        (grad_atmos, grad_ocean, grad_project, grad_inject), ("lon", "lat")
    )
    return (ocean_out, grad_atmos, grad_ocean, grad_project, grad_inject)


def solution(mesh):
    return jax.shard_map(
        body,
        mesh=mesh,
        in_specs=(
            P("lat", "lon", None),
            P(),
            P(),
            P("lat", "lon", None),
            P("lat", "lon", None),
            P("lat", "lon", None),
            P("lat", "lon", None),
            P(),
            P("lat", "lon"),
            P(),
            P("lat", "lon", None),
        ),
        out_specs=(P("lat", "lon", None), P(), P(), P(), P()),
        check_vma=False,
    )
```

profile of v0, /device:TPU:1, one launch (start us, length us, event | category | flops | bytes accessed | tf_op | source)
XLA Modules:
  0.0 516.5 jit_solution(17819121093324775576)
XLA Ops:
  8.0 4.5 collective-permute-start
  14.5 3.3 collective-permute-done.1
  20.1 3.0 collective-permute-start.2
  23.1 3.6 collective-permute-start.3
  27.9 3.8 pad_maximum_fusion.11
  40.4 5.2 %collective-permute-start.5 = (bf16[32,4096]{1,0:T(8,128)(2,1)S(1)}, bf16[32,4096]{1,0:T(8,128)(2,1)S(1)}, u32[]{:S(2)}, u32[]{:S(2)}) collective-permute-start(bf16[32,4096]{1,0:T(8,128)(2,1)S(1)} %reshape.233), channel_id=1, source_target_pairs={{0,112},{16,0},{32,16},{48,32},{64,48},{80,64},{96,80},{112,96},{1... | collective-permute-start | bytes 786440 | tf_op jit(solution)/shard_map/ppermute | solution.py:15
  46.1 5.6 %collective-permute-done.5 = bf16[32,4096]{1,0:T(8,128)(2,1)S(1)} collective-permute-done((bf16[32,4096]{1,0:T(8,128)(2,1)S(1)}, bf16[32,4096]{1,0:T(8,128)(2,1)S(1)}, u32[]{:S(2)}, u32[]{:S(2)}) %collective-permute-start.5) | collective-permute-done | bytes 262176 | tf_op jit(solution)/shard_map/ppermute | solution.py:15
  51.7 6.7 %collective-permute-done.4 = bf16[32,4096]{1,0:T(8,128)(2,1)S(1)} collective-permute-done((bf16[32,4096]{1,0:T(8,128)(2,1)S(1)}, bf16[32,4096]{1,0:T(8,128)(2,1)S(1)}, u32[]{:S(2)}, u32[]{:S(2)}) %collective-permute-start.4) | collective-permute-done | bytes 262176 | tf_op jit(solution)/shard_map/ppermute | solution.py:15
  61.7 3.7 collective-permute-start.6
  76.9 6.2 %reshape.234 = bf16[18432,64]{1,0:T(8,128)(2,1)} reshape(bf16[3,3,32,4096]{3,2,1,0:T(8,128)(2,1)S(1)} %pad_maximum_fusion) | data formatting | bytes 4718592 | tf_op jit(solution)/shard_map/reshape | solution.py:129
  83.1 31.3 %gather_fusion = bf16[8192,64]{1,0:T(8,128)(2,1)} fusion(bf16[18432,64]{1,0:T(8,128)(2,1)} %reshape.234, s32[8192]{0:T(1024)S(1)} %broadcast_clamp_fusion), kind=kCustom, calls=%fused_computation | custom fusion | bytes 2129920 | tf_op jit(solution)/shard_map/jit(_take)/gather | solution.py:139
  114.4 6.9 %multiply_reduce_fusion = bf16[32,64,64]{2,1,0:T(8,128)(2,1)S(1)} fusion(bf16[32,64,4,64]{3,2,1,0:T(4,128)(2,1)} %bitcast.318, f32[32,64,4]{2,1,0:T(8,128)S(1)} %copy-done.20, pred[32,64,4]{2,1,0:T(8,128)(4,1)S(1)} %copy-done.36), kind=kLoop, calls=%fused_computation.5 | loop fusion | flops 1966080 | bytes 1351680 | tf_op jit(solution)/shard_map/reduce_sum | solution.py:141
  132.8 6.1 %collective-permute-start.8 = (bf16[1,64,256]{2,1,0:T(8,128)(2,1)S(1)}, bf16[1,64,256]{2,1,0:T(8,128)(2,1)S(1)}, u32[]{:S(2)}, u32[]{:S(2)}) collective-permute-start(bf16[1,64,256]{2,1,0:T(8,128)(2,1)S(1)} %get-tuple-element.67), channel_id=1, source_target_pairs={{0,1},{1,2},{2,3},{3,4},{4,5},{5,6},{6,7},{7,8},{8,9},{9,10},{10,1... | collective-permute-start | bytes 98312 | tf_op jit(solution)/shard_map/ppermute | solution.py:10
  139.9 4.5 collective-permute-start.14
  145.5 5.5 %collective-permute-done.13 = bf16[34,1,256]{2,1,0:T(2,128)(2,1)S(1)} collective-permute-done((bf16[34,1,256]{2,1,0:T(2,128)(2,1)S(1)}, bf16[34,1,256]{2,1,0:T(2,128)(2,1)S(1)}, u32[]{:S(2)}, u32[]{:S(2)}) %collective-permute-start.13) | collective-permute-done | bytes 17440 | tf_op jit(solution)/shard_map/ppermute | solution.py:15
  159.7 5.6 %collective-permute-start.15 = (bf16[1,64,256]{2,1,0:T(8,128)(2,1)S(1)}, bf16[1,64,256]{2,1,0:T(8,128)(2,1)S(1)}, u32[]{:S(2)}, u32[]{:S(2)}) collective-permute-start(bf16[1,64,256]{2,1,0:T(8,128)(2,1)S(1)} %get-tuple-element.63), channel_id=1, source_target_pairs={{0,1},{1,2},{2,3},{3,4},{4,5},{5,6},{6,7},{7,8},{8,9},{9,10},{10,1... | collective-permute-start | bytes 98312 | tf_op jit(solution)/shard_map/ppermute | solution.py:10
  174.7 3.3 collective-permute-done.18
  179.6 2.7 collective-permute-start.21
  184.4 4.7 collective-permute-done.20
  203.7 4.0 mul.113
  207.7 52.9 %scatter_custom_fusion = f32[18432,64]{1,0:T(8,128)} fusion(s32[8192]{0:T(1024)} %bitcast.345, f32[]{:T(128)} %constant.131.clone.1, f32[8192,64]{1,0:T(8,128)} %bitcast.301, f32[8192]{0:T(1024)S(1)} %mul.106), kind=kCustom, calls=%fused_computation.2 | custom fusion | flops 1048576 | bytes 8946176 | tf_op jit(solution)/shard_map/scatter-add | solution.py:170
  260.6 4.3 convert_element_type.85
  267.1 3.2 squeeze.109
  270.3 3.2 squeeze.110
  275.6 6.5 %collective-permute-start.22 = (bf16[3,32,4096]{2,1,0:T(8,128)(2,1)}, bf16[3,32,4096]{2,1,0:T(8,128)(2,1)}, u32[]{:S(2)}, u32[]{:S(2)}) collective-permute-start(bf16[3,32,4096]{2,1,0:T(8,128)(2,1)} %squeeze.109), channel_id=1, source_target_pairs={{0,1},{1,2},{2,3},{3,4},{4,5},{5,6},{6,7},{7,8},{8,9},{9,10},{10,1... | collective-permute-start | bytes 2359304 | tf_op jit(solution)/shard_map/ppermute | solution.py:10
  285.6 2.4 slice.348
  293.1 2.9 collective-permute-start.25
  299.5 20.1 %collective-permute-done.24 = bf16[3,32,4096]{2,1,0:T(8,128)(2,1)S(1)} collective-permute-done((bf16[3,32,4096]{2,1,0:T(8,128)(2,1)S(1)}, bf16[3,32,4096]{2,1,0:T(8,128)(2,1)S(1)}, u32[]{:S(2)}, u32[]{:S(2)}) %collective-permute-start.24) | collective-permute-done | bytes 786464 | tf_op jit(solution)/shard_map/ppermute | solution.py:15
  319.8 12.5 %collective-permute-done.25 = bf16[3,32,4096]{2,1,0:T(8,128)(2,1)S(1)} collective-permute-done((bf16[3,32,4096]{2,1,0:T(8,128)(2,1)S(1)}, bf16[3,32,4096]{2,1,0:T(8,128)(2,1)S(1)}, u32[]{:S(2)}, u32[]{:S(2)}) %collective-permute-start.25) | collective-permute-done | bytes 786464 | tf_op jit(solution)/shard_map/ppermute | solution.py:15
  334.0 2.5 fusion.6
  344.1 159.4 %all-reduce.3.cloned.1.call-done = (f32[9,256,256]{2,1,0:T(8,128)}, f32[9,256,256]{2,1,0:T(8,128)}, f32[256,64]{0,1:T(8,128)}, f32[64,256]{1,0:T(8,128)}) async-done(((f32[9,256,256]{2,1,0:T(8,128)}, f32[9,256,256]{2,1,0:T(8,128)}, f32[256,64]{0,1:T(8,128)}, f32[64,256]{1,0:T(8,128)}), (f32[9,256,256]{2,1,0:T(8,128)}, f32[9,256,256]{2,1,0:T(8,128)}, f32[256,64]{0,1:T(8,128)}, ...) | async-done | bytes 4849680 | tf_op jit(solution)/shard_map/psum | solution.py:186
  503.5 3.4 copy.67
  (234 shorter events, 107.8 us)
Async XLA Ops:
  7.2 115.0 %copy-start = (bf16[64,256]{1,0:T(8,128)(2,1)S(1)}, bf16[64,256]{1,0:T(8,128)(2,1)}, u32[]{:S(2)}) copy-start(bf16[64,256]{1,0:T(8,128)(2,1)} %param.20) | copy-start | bytes 98308
  7.2 496.3 %all-reduce.3.cloned.1.call-start = ((), (), s32[]{:S(2)}) async-start(), calls=%async_computation | async-start | bytes 9699328 | tf_op jit(solution)/shard_map/psum | solution.py:186
  8.0 6.4 %collective-permute-start = (bf16[1,64,256]{2,1,0:T(8,128)(2,1)S(1)}, bf16[1,64,256]{2,1,0:T(8,128)(2,1)S(1)}, u32[]{:S(2)}, u32[]{:S(2)}) collective-permute-start(bf16[1,64,256]{2,1,0:T(8,128)(2,1)S(1)} %get-tuple-element.72), channel_id=1, source_target_pairs={{0,1},{1,2},{2,3},{3,4},{4,5},{5,6},{6,7},{7,8},{8,9},{9,10},{10,1... | collective-permute-start | bytes 98312 | tf_op jit(solution)/shard_map/ppermute | solution.py:10
  12.5 5.2 %collective-permute-start.1 = (bf16[1,64,256]{2,1,0:T(8,128)(2,1)S(1)}, bf16[1,64,256]{2,1,0:T(8,128)(2,1)S(1)}, u32[]{:S(2)}, u32[]{:S(2)}) collective-permute-start(bf16[1,64,256]{2,1,0:T(8,128)(2,1)S(1)} %get-tuple-element.71), channel_id=1, source_target_pairs={{1,0},{2,1},{3,2},{4,3},{5,4},{6,5},{7,6},{8,7},{9,8},{10,9},{11,1... | collective-permute-start | bytes 98312 | tf_op jit(solution)/shard_map/ppermute | solution.py:10
  20.1 7.8 %collective-permute-start.2 = (bf16[34,1,256]{2,1,0:T(2,128)(2,1)S(1)}, bf16[34,1,256]{2,1,0:T(2,128)(2,1)S(1)}, u32[]{:S(2)}, u32[]{:S(2)}) collective-permute-start(bf16[34,1,256]{2,1,0:T(2,128)(2,1)S(1)} %get-tuple-element.60), channel_id=1, source_target_pairs={{0,16},{16,32},{32,48},{48,64},{64,80},{80,96},{96,112},{112,0},{1... | collective-permute-start | bytes 52232 | tf_op jit(solution)/shard_map/ppermute | solution.py:15
  23.1 4.8 collective-permute-start.3
  39.9 25.5 %copy-start.44 = (s32[32,64]{1,0:T(8,128)S(1)}, s32[32,64]{1,0:T(8,128)}, u32[]{:S(2)}) copy-start(s32[32,64]{1,0:T(8,128)} %param.21) | copy-start | bytes 24580
  40.4 11.3 %collective-permute-start.5 = (bf16[32,4096]{1,0:T(8,128)(2,1)S(1)}, bf16[32,4096]{1,0:T(8,128)(2,1)S(1)}, u32[]{:S(2)}, u32[]{:S(2)}) collective-permute-start(bf16[32,4096]{1,0:T(8,128)(2,1)S(1)} %reshape.233), channel_id=1, source_target_pairs={{0,112},{16,0},{32,16},{48,32},{64,48},{80,64},{96,80},{112,96},{1... | collective-permute-start | bytes 786440 | tf_op jit(solution)/shard_map/ppermute | solution.py:15
  45.6 12.8 %collective-permute-start.4 = (bf16[32,4096]{1,0:T(8,128)(2,1)S(1)}, bf16[32,4096]{1,0:T(8,128)(2,1)S(1)}, u32[]{:S(2)}, u32[]{:S(2)}) collective-permute-start(bf16[32,4096]{1,0:T(8,128)(2,1)S(1)} %reshape.233), channel_id=1, source_target_pairs={{0,16},{16,32},{32,48},{48,64},{64,80},{80,96},{96,112},{112,0},{1... | collective-permute-start | bytes 786440 | tf_op jit(solution)/shard_map/ppermute | solution.py:15
  59.4 13.6 %collective-permute-start.7 = (bf16[3,32,4096]{2,1,0:T(8,128)(2,1)S(1)}, bf16[3,32,4096]{2,1,0:T(8,128)(2,1)S(1)}, u32[]{:S(2)}, u32[]{:S(2)}) collective-permute-start(bf16[3,32,4096]{2,1,0:T(8,128)(2,1)S(1)} %get-tuple-element.74), channel_id=1, source_target_pairs={{1,0},{2,1},{3,2},{4,3},{5,4},{6,5},{7,6},{8,7},{9,8},{10,9},{11,1... | collective-permute-start | bytes 2359304 | tf_op jit(solution)/shard_map/ppermute | solution.py:10
  61.7 12.5 %collective-permute-start.6 = (bf16[3,32,4096]{2,1,0:T(8,128)(2,1)S(1)}, bf16[3,32,4096]{2,1,0:T(8,128)(2,1)S(1)}, u32[]{:S(2)}, u32[]{:S(2)}) collective-permute-start(bf16[3,32,4096]{2,1,0:T(8,128)(2,1)S(1)} %get-tuple-element.74), channel_id=1, source_target_pairs={{0,1},{1,2},{2,3},{3,4},{4,5},{5,6},{6,7},{7,8},{8,9},{9,10},{10,1... | collective-permute-start | bytes 2359304 | tf_op jit(solution)/shard_map/ppermute | solution.py:10
  83.1 31.3 %copy-start.20 = (f32[32,64,4]{2,1,0:T(8,128)S(1)}, f32[32,64,4]{2,1,0:T(8,128)}, u32[]{:S(2)}) copy-start(f32[32,64,4]{2,1,0:T(8,128)} %copy.31) | copy-start | bytes 98308
  83.1 31.3 %copy-start.36 = (pred[32,64,4]{2,1,0:T(8,128)(4,1)S(1)}, pred[32,64,4]{2,1,0:T(8,128)(4,1)}, u32[]{:S(2)}) copy-start(pred[32,64,4]{2,1,0:T(8,128)(4,1)} %copy.32) | copy-start | bytes 24580
  122.7 4.3 collective-permute-start.9
  127.0 3.1 collective-permute-start.10
  128.2 10.8 %collective-permute-start.12 = (bf16[1,64,256]{2,1,0:T(8,128)(2,1)S(1)}, bf16[1,64,256]{2,1,0:T(8,128)(2,1)S(1)}, u32[]{:S(2)}, u32[]{:S(2)}) collective-permute-start(bf16[1,64,256]{2,1,0:T(8,128)(2,1)S(1)} %get-tuple-element.66), channel_id=1, source_target_pairs={{1,0},{2,1},{3,2},{4,3},{5,4},{6,5},{7,6},{8,7},{9,8},{10,9},{11,1... | collective-permute-start | bytes 98312 | tf_op jit(solution)/shard_map/ppermute | solution.py:10
  130.1 8.8 %collective-permute-start.11 = (bf16[1,64,256]{2,1,0:T(8,128)(2,1)S(1)}, bf16[1,64,256]{2,1,0:T(8,128)(2,1)S(1)}, u32[]{:S(2)}, u32[]{:S(2)}) collective-permute-start(bf16[1,64,256]{2,1,0:T(8,128)(2,1)S(1)} %collective-permute-done.10), channel_id=1, source_target_pairs={{0,64},{16,80},{32,96},{48,112},{64,0},{80,16},{96,32},{112,48},{1... | collective-permute-start | bytes 98312 | tf_op jit(solution)/shard_map/ppermute | solution.py:19
  132.8 7.1 %collective-permute-start.8 = (bf16[1,64,256]{2,1,0:T(8,128)(2,1)S(1)}, bf16[1,64,256]{2,1,0:T(8,128)(2,1)S(1)}, u32[]{:S(2)}, u32[]{:S(2)}) collective-permute-start(bf16[1,64,256]{2,1,0:T(8,128)(2,1)S(1)} %get-tuple-element.67), channel_id=1, source_target_pairs={{0,1},{1,2},{2,3},{3,4},{4,5},{5,6},{6,7},{7,8},{8,9},{9,10},{10,1... | collective-permute-start | bytes 98312 | tf_op jit(solution)/shard_map/ppermute | solution.py:10
  139.9 5.5 %collective-permute-start.14 = (bf16[34,1,256]{2,1,0:T(2,128)(2,1)S(1)}, bf16[34,1,256]{2,1,0:T(2,128)(2,1)S(1)}, u32[]{:S(2)}, u32[]{:S(2)}) collective-permute-start(bf16[34,1,256]{2,1,0:T(2,128)(2,1)S(1)} %get-tuple-element.55), channel_id=1, source_target_pairs={{0,112},{16,0},{32,16},{48,32},{64,48},{80,64},{96,80},{112,96},{1... | collective-permute-start | bytes 52232 | tf_op jit(solution)/shard_map/ppermute | solution.py:15
  144.4 6.6 %collective-permute-start.13 = (bf16[34,1,256]{2,1,0:T(2,128)(2,1)S(1)}, bf16[34,1,256]{2,1,0:T(2,128)(2,1)S(1)}, u32[]{:S(2)}, u32[]{:S(2)}) collective-permute-start(bf16[34,1,256]{2,1,0:T(2,128)(2,1)S(1)} %get-tuple-element.56), channel_id=1, source_target_pairs={{0,16},{16,32},{32,48},{48,64},{64,80},{80,96},{96,112},{112,0},{1... | collective-permute-start | bytes 52232 | tf_op jit(solution)/shard_map/ppermute | solution.py:15
  151.9 17.7 %copy-start.1 = (bf16[34,65,256]{2,1,0:T(8,128)(2,1)}, bf16[34,65,256]{2,1,0:T(8,128)(2,1)S(1)}, u32[]{:S(2)}) copy-start(bf16[34,65,256]{2,1,0:T(8,128)(2,1)S(1)} %get-tuple-element.53) | copy-start | bytes 3394564
  159.7 11.1 %collective-permute-start.16 = (bf16[1,64,256]{2,1,0:T(8,128)(2,1)S(1)}, bf16[1,64,256]{2,1,0:T(8,128)(2,1)S(1)}, u32[]{:S(2)}, u32[]{:S(2)}) collective-permute-start(bf16[1,64,256]{2,1,0:T(8,128)(2,1)S(1)} %get-tuple-element.63), channel_id=1, source_target_pairs={{0,16},{16,0},{32,48},{48,32},{64,80},{80,64},{96,112},{112,96},{1... | collective-permute-start | bytes 98312 | tf_op jit(solution)/shard_map/ppermute | solution.py:19
  159.7 14.0 %collective-permute-start.15 = (bf16[1,64,256]{2,1,0:T(8,128)(2,1)S(1)}, bf16[1,64,256]{2,1,0:T(8,128)(2,1)S(1)}, u32[]{:S(2)}, u32[]{:S(2)}) collective-permute-start(bf16[1,64,256]{2,1,0:T(8,128)(2,1)S(1)} %get-tuple-element.63), channel_id=1, source_target_pairs={{0,1},{1,2},{2,3},{3,4},{4,5},{5,6},{6,7},{7,8},{8,9},{9,10},{10,1... | collective-permute-start | bytes 98312 | tf_op jit(solution)/shard_map/ppermute | solution.py:10
  166.5 12.3 %collective-permute-start.19 = (bf16[1,64,256]{2,1,0:T(8,128)(2,1)}, bf16[1,64,256]{2,1,0:T(8,128)(2,1)}, u32[]{:S(2)}, u32[]{:S(2)}) collective-permute-start(bf16[1,64,256]{2,1,0:T(8,128)(2,1)} %get-tuple-element.62), channel_id=1, source_target_pairs={{1,0},{2,1},{3,2},{4,3},{5,4},{6,5},{7,6},{8,7},{9,8},{10,9},{11,1... | collective-permute-start | bytes 98312 | tf_op jit(solution)/shard_map/ppermute | solution.py:10
  170.8 2.8 collective-permute-start.17
  173.6 4.4 collective-permute-start.18
  179.6 4.8 collective-permute-start.21
  182.3 6.8 %collective-permute-start.20 = (bf16[34,1,256]{2,1,0:T(2,128)(2,1)S(1)}, bf16[34,1,256]{2,1,0:T(2,128)(2,1)S(1)}, u32[]{:S(2)}, u32[]{:S(2)}) collective-permute-start(bf16[34,1,256]{2,1,0:T(2,128)(2,1)S(1)} %get-tuple-element.52), channel_id=1, source_target_pairs={{0,16},{16,32},{32,48},{48,64},{64,80},{80,96},{96,112},{112,0},{1... | collective-permute-start | bytes 52232 | tf_op jit(solution)/shard_map/ppermute | solution.py:15
  273.5 16.6 %collective-permute-start.23 = (bf16[3,32,4096]{2,1,0:T(8,128)(2,1)}, bf16[3,32,4096]{2,1,0:T(8,128)(2,1)}, u32[]{:S(2)}, u32[]{:S(2)}) collective-permute-start(bf16[3,32,4096]{2,1,0:T(8,128)(2,1)} %squeeze.110), channel_id=1, source_target_pairs={{1,0},{2,1},{3,2},{4,3},{5,4},{6,5},{7,6},{8,7},{9,8},{10,9},{11,1... | collective-permute-start | bytes 2359304 | tf_op jit(solution)/shard_map/ppermute | solution.py:10
  275.6 15.7 %collective-permute-start.22 = (bf16[3,32,4096]{2,1,0:T(8,128)(2,1)}, bf16[3,32,4096]{2,1,0:T(8,128)(2,1)}, u32[]{:S(2)}, u32[]{:S(2)}) collective-permute-start(bf16[3,32,4096]{2,1,0:T(8,128)(2,1)} %squeeze.109), channel_id=1, source_target_pairs={{0,1},{1,2},{2,3},{3,4},{4,5},{5,6},{6,7},{7,8},{8,9},{9,10},{10,1... | collective-permute-start | bytes 2359304 | tf_op jit(solution)/shard_map/ppermute | solution.py:10
  293.0 26.6 %collective-permute-start.24 = (bf16[3,32,4096]{2,1,0:T(8,128)(2,1)S(1)}, bf16[3,32,4096]{2,1,0:T(8,128)(2,1)S(1)}, u32[]{:S(2)}, u32[]{:S(2)}) collective-permute-start(bf16[3,32,4096]{2,1,0:T(8,128)(2,1)S(1)} %get-tuple-element.26), channel_id=1, source_target_pairs={{0,112},{16,0},{32,16},{48,32},{64,48},{80,64},{96,80},{112,96},{1... | collective-permute-start | bytes 2359304 | tf_op jit(solution)/shard_map/ppermute | solution.py:15
  293.1 39.1 %collective-permute-start.25 = (bf16[3,32,4096]{2,1,0:T(8,128)(2,1)S(1)}, bf16[3,32,4096]{2,1,0:T(8,128)(2,1)S(1)}, u32[]{:S(2)}, u32[]{:S(2)}) collective-permute-start(bf16[3,32,4096]{2,1,0:T(8,128)(2,1)S(1)} %get-tuple-element.27), channel_id=1, source_target_pairs={{0,16},{16,32},{32,48},{48,64},{64,80},{80,96},{96,112},{112,0},{1... | collective-permute-start | bytes 2359304 | tf_op jit(solution)/shard_map/ppermute | solution.py:15
  (40 other events, 128.8 us)
Sparse Core Ops, SparseCore 0:
  344.2 159.2 all-reduce.2
where the time goes:
time: 524 us; the launch traced here: 517 us
  waiting for transfers between devices  231 us (44%)
  other arithmetic  85.4 us (16%)
  local copies, waits for them, and re-layouts  84.4 us (16%)
  starting transfers between devices  63.3 us (12%)
  matrix products  36.9 us (7%)
  between operations  15.2 us (3%)
    psum x1, waiting for transfers between devices, body(): lax.psum((grad_atmos, grad_ocean, grad_project, grad_inject), ('lon', 'la...  159 us
    ppermute x10, waiting for transfers between devices, shifted(): lax.ppermute(x, axis, [(i, (i + by) % length) for i in range(length)])  55.8 us
    scatter-add x1, other arithmetic, body(): credit = jnp.zeros((9 * cells, flux_chans), jnp.float32).at[slots.reshape...  52.9 us
    ppermute x10, starting transfers between devices, passed_along(): return lax.ppermute(x, axis, pairs)  36.5 us
    gather x1, local copies, waits for them, and re-layouts, body(): picked = jnp.take(neighbourhood, slots, axis=0).astype(jnp.float32)  31.3 us
    ppermute x10, starting transfers between devices, shifted(): lax.ppermute(x, axis, [(i, (i + by) % length) for i in range(length)])  23.2 us
    unnamed x97, local copies, waits for them, and re-layouts  18.9 us
    dot_general x18, matrix products, kernel_grads(): jnp.einsum('nc,nd->cd', window, delta, preferred_element_type=jnp.float32)  15.1 us
  transfers between devices with their start and end apart: 27, of which 18 were waited for; matrix products, arithmetic and copies ran while one was open for 6% of the time, Pallas kernels for 0%

commit v1 on v0

--- a/solution.py
+++ b/solution.py
@@ -184,7 +184,7 @@
     atmos_delta = (act_grad * silu_slope(atmos_pre)).astype(jnp.bfloat16)
     grad_atmos = kernel_grads(atmos_padded, atmos_delta, row_count, col_count)
     grad_atmos, grad_ocean, grad_project, grad_inject = lax.psum(
-        (grad_atmos, grad_ocean, grad_project, grad_inject), ("lon", "lat")
+        lax.psum((grad_atmos, grad_ocean, grad_project, grad_inject), "lat"), "lon"
     )
     return (ocean_out, grad_atmos, grad_ocean, grad_project, grad_inject)
 

time: 524 us -> 707 us (1.35)
  waiting for transfers between devices: 231 us -> 427 us
  local copies, waits for them, and re-layouts: 84.4 us -> 75 us
    psum x1 -> x2, waiting for transfers between devices: 159 us -> 350 us  [the longest x1 216 us: body(): lax.psum(lax.psum((grad_atmos, grad_ocean, grad_project, grad_inject), 'l...]
    unnamed x97 -> x101, local copies, waits for them, and re-layouts: 18.9 us -> 16.1 us
  transfers between devices with their start and end apart: 27 -> 28, of which waited for: 18 -> 19; matrix products, arithmetic and copies ran while one was open for 6% -> 4% of each run, Pallas kernels for 0% -> 0%
where the time goes in v1:
time: 707 us; the launch traced here: 700 us
  waiting for transfers between devices  427 us (60%)
  other arithmetic  82.3 us (12%)
  local copies, waits for them, and re-layouts  75 us (11%)
  starting transfers between devices  63.4 us (9%)
  matrix products  37 us (5%)
  between operations  15.3 us (2%)
    psum x1, waiting for transfers between devices, body(): lax.psum(lax.psum((grad_atmos, grad_ocean, grad_project, grad_inject), 'l...  216 us
    psum x1, waiting for transfers between devices, body(): lax.psum((grad_atmos, grad_ocean, grad_project, grad_inject), 'lat')  134 us
    ppermute x10, waiting for transfers between devices, shifted(): lax.ppermute(x, axis, [(i, (i + by) % length) for i in range(length)])  55.7 us
    scatter-add x1, other arithmetic, body(): credit = jnp.zeros((9 * cells, flux_chans), jnp.float32).at[slots.reshape...  52.9 us
    ppermute x10, starting transfers between devices, passed_along(): return lax.ppermute(x, axis, pairs)  36.5 us
    gather x1, local copies, waits for them, and re-layouts, body(): picked = jnp.take(neighbourhood, slots, axis=0).astype(jnp.float32)  24.9 us
    ppermute x10, starting transfers between devices, shifted(): lax.ppermute(x, axis, [(i, (i + by) % length) for i in range(length)])  23.2 us
    unnamed x101, local copies, waits for them, and re-layouts  16.1 us
  transfers between devices with their start and end apart: 28, of which 19 were waited for; matrix products, arithmetic and copies ran while one was open for 4% of the time, Pallas kernels for 0%

profile of v1, /device:TPU:1, one launch (start us, length us, event | category | flops | bytes accessed | tf_op | source)
XLA Modules:
  0.0 699.6 jit_solution(5898172512244059729)
XLA Ops:
  8.0 4.5 collective-permute-start
  14.5 3.3 collective-permute-done.1
  20.1 3.0 collective-permute-start.2
  23.1 3.6 collective-permute-start.3
  27.9 3.8 pad_maximum_fusion.11
  40.5 5.2 collective-permute-start.5
  46.2 5.6 collective-permute-done.5
  51.8 6.7 collective-permute-done.4
  62.0 3.7 collective-permute-start.6
  68.8 4.7 collective-permute-done.7
  76.7 6.1 reshape.234
  82.8 24.9 %gather_fusion = bf16[8192,64]{1,0:T(8,128)(2,1)S(1)} fusion(bf16[18432,64]{1,0:T(8,128)(2,1)} %reshape.234, s32[8192]{0:T(1024)S(1)} %broadcast_clamp_fusion), kind=kCustom, calls=%fused_computation | custom fusion | bytes 2129920 | tf_op jit(solution)/shard_map/jit(_take)/gather | solution.py:139
  107.7 5.9 multiply_reduce_fusion
  125.6 6.1 collective-permute-start.8
  132.8 4.5 collective-permute-start.14
  138.3 5.5 collective-permute-done.13
  152.5 5.6 collective-permute-start.15
  167.5 3.3 collective-permute-done.18
  171.7 2.7 collective-permute-start.21
  176.5 4.7 collective-permute-done.20
  195.7 4.1 mul.113
  199.8 52.9 %scatter_custom_fusion = f32[18432,64]{1,0:T(8,128)} fusion(s32[8192]{0:T(1024)} %bitcast.344, f32[]{:T(128)} %constant.131.clone.1, f32[8192,64]{1,0:T(8,128)} %bitcast.301, f32[8192]{0:T(1024)S(1)} %copy-done.38), kind=kCustom, calls=%fused_computation.2 | custom fusion | flops 1048576 | bytes 8946176 | tf_op jit(solution)/shard_map/scatter-add | solution.py:170
  252.7 4.3 convert_element_type.85
  259.2 3.2 squeeze.109
  262.4 3.2 squeeze.110
  267.7 6.5 collective-permute-start.22
  285.2 2.9 collective-permute-start.25
  291.6 20.1 %collective-permute-done.24 = bf16[3,32,4096]{2,1,0:T(8,128)(2,1)S(1)} collective-permute-done((bf16[3,32,4096]{2,1,0:T(8,128)(2,1)S(1)}, bf16[3,32,4096]{2,1,0:T(8,128)(2,1)S(1)}, u32[]{:S(2)}, u32[]{:S(2)}) %collective-permute-start.24) | collective-permute-done | bytes 786464 | tf_op jit(solution)/shard_map/ppermute | solution.py:15
  311.9 12.5 %collective-permute-done.25 = bf16[3,32,4096]{2,1,0:T(8,128)(2,1)S(1)} collective-permute-done((bf16[3,32,4096]{2,1,0:T(8,128)(2,1)S(1)}, bf16[3,32,4096]{2,1,0:T(8,128)(2,1)S(1)}, u32[]{:S(2)}, u32[]{:S(2)}) %collective-permute-start.25) | collective-permute-done | bytes 786464 | tf_op jit(solution)/shard_map/ppermute | solution.py:15
  336.2 134.3 %all-reduce.5.cloned.1.call-done = (f32[9,256,256]{2,1,0:T(8,128)}, f32[9,256,256]{2,1,0:T(8,128)}, f32[256,64]{0,1:T(8,128)}, f32[64,256]{1,0:T(8,128)}) async-done(((f32[9,256,256]{2,1,0:T(8,128)}, f32[9,256,256]{2,1,0:T(8,128)}, f32[256,64]{0,1:T(8,128)}, f32[64,256]{1,0:T(8,128)}), (f32[9,256,256]{2,1,0:T(8,128)}, f32[9,256,256]{2,1,0:T(8,128)}, f32[256,64]{0,1:T(8,128)}, ...) | async-done | bytes 4849680 | tf_op jit(solution)/shard_map/psum | solution.py:187
  470.5 216.0 %all-reduce.7.cloned.1.call-done = (f32[9,256,256]{2,1,0:T(8,128)}, f32[9,256,256]{2,1,0:T(8,128)}, f32[256,64]{0,1:T(8,128)}, f32[64,256]{1,0:T(8,128)}) async-done(((f32[9,256,256]{2,1,0:T(8,128)}, f32[9,256,256]{2,1,0:T(8,128)}, f32[256,64]{0,1:T(8,128)}, f32[64,256]{1,0:T(8,128)}), (f32[9,256,256]{2,1,0:T(8,128)}, f32[9,256,256]{2,1,0:T(8,128)}, f32[256,64]{0,1:T(8,128)}, ...) | async-done | bytes 4849680 | tf_op jit(solution)/shard_map/psum | solution.py:186
  686.5 3.4 copy.71
  (241 shorter events, 107.5 us)
Async XLA Ops:
  7.2 107.2 %copy-start = (bf16[64,256]{1,0:T(8,128)(2,1)S(1)}, bf16[64,256]{1,0:T(8,128)(2,1)}, u32[]{:S(2)}) copy-start(bf16[64,256]{1,0:T(8,128)(2,1)} %param.20) | copy-start | bytes 98308
  7.2 463.3 %all-reduce.5.cloned.1.call-start = ((), (), s32[]{:S(2)}) async-start(), calls=%async_computation | async-start | bytes 9699328 | tf_op jit(solution)/shard_map/psum | solution.py:187
  8.0 6.4 collective-permute-start
  12.5 5.2 collective-permute-start.1
  20.1 7.8 %collective-permute-start.2 = (bf16[34,1,256]{2,1,0:T(2,128)(2,1)S(1)}, bf16[34,1,256]{2,1,0:T(2,128)(2,1)S(1)}, u32[]{:S(2)}, u32[]{:S(2)}) collective-permute-start(bf16[34,1,256]{2,1,0:T(2,128)(2,1)S(1)} %get-tuple-element.64), channel_id=1, source_target_pairs={{0,16},{16,32},{32,48},{48,64},{64,80},{80,96},{96,112},{112,0},{1... | collective-permute-start | bytes 52232 | tf_op jit(solution)/shard_map/ppermute | solution.py:15
  23.1 4.8 collective-permute-start.3
  40.0 25.8 %copy-start.46 = (s32[32,64]{1,0:T(8,128)S(1)}, s32[32,64]{1,0:T(8,128)}, u32[]{:S(2)}) copy-start(s32[32,64]{1,0:T(8,128)} %param.21) | copy-start | bytes 24580
  40.0 25.8 %copy-start.40 = (s32[32,64,4]{1,2,0:T(4,128)S(1)}, s32[32,64,4]{1,2,0:T(4,128)}, u32[]{:S(2)}) copy-start(s32[32,64,4]{1,2,0:T(4,128)} %param.17) | copy-start | bytes 98308
  40.0 25.8 %copy-start.41 = (s32[32,64,4]{1,2,0:T(4,128)S(1)}, s32[32,64,4]{1,2,0:T(4,128)}, u32[]{:S(2)}) copy-start(s32[32,64,4]{1,2,0:T(4,128)} %param.16) | copy-start | bytes 98308
  40.5 11.3 %collective-permute-start.5 = (bf16[32,4096]{1,0:T(8,128)(2,1)S(1)}, bf16[32,4096]{1,0:T(8,128)(2,1)S(1)}, u32[]{:S(2)}, u32[]{:S(2)}) collective-permute-start(bf16[32,4096]{1,0:T(8,128)(2,1)S(1)} %reshape.233), channel_id=1, source_target_pairs={{0,112},{16,0},{32,16},{48,32},{64,48},{80,64},{96,80},{112,96},{1... | collective-permute-start | bytes 786440 | tf_op jit(solution)/shard_map/ppermute | solution.py:15
  45.7 12.8 %collective-permute-start.4 = (bf16[32,4096]{1,0:T(8,128)(2,1)S(1)}, bf16[32,4096]{1,0:T(8,128)(2,1)S(1)}, u32[]{:S(2)}, u32[]{:S(2)}) collective-permute-start(bf16[32,4096]{1,0:T(8,128)(2,1)S(1)} %reshape.233), channel_id=1, source_target_pairs={{0,16},{16,32},{32,48},{48,64},{64,80},{80,96},{96,112},{112,0},{1... | collective-permute-start | bytes 786440 | tf_op jit(solution)/shard_map/ppermute | solution.py:15
  59.7 13.8 %collective-permute-start.7 = (bf16[3,32,4096]{2,1,0:T(8,128)(2,1)}, bf16[3,32,4096]{2,1,0:T(8,128)(2,1)S(1)}, u32[]{:S(2)}, u32[]{:S(2)}) collective-permute-start(bf16[3,32,4096]{2,1,0:T(8,128)(2,1)} %get-tuple-element.78), channel_id=1, source_target_pairs={{1,0},{2,1},{3,2},{4,3},{5,4},{6,5},{7,6},{8,7},{9,8},{10,9},{11,1... | collective-permute-start | bytes 2359304 | tf_op jit(solution)/shard_map/ppermute | solution.py:10
  62.0 12.8 %collective-permute-start.6 = (bf16[3,32,4096]{2,1,0:T(8,128)(2,1)}, bf16[3,32,4096]{2,1,0:T(8,128)(2,1)}, u32[]{:S(2)}, u32[]{:S(2)}) collective-permute-start(bf16[3,32,4096]{2,1,0:T(8,128)(2,1)} %get-tuple-element.78), channel_id=1, source_target_pairs={{0,1},{1,2},{2,3},{3,4},{4,5},{5,6},{6,7},{7,8},{8,9},{9,10},{10,1... | collective-permute-start | bytes 2359304 | tf_op jit(solution)/shard_map/ppermute | solution.py:10
  114.9 4.3 collective-permute-start.9
  119.2 3.1 collective-permute-start.10
  120.4 11.4 %collective-permute-start.12 = (bf16[1,64,256]{2,1,0:T(8,128)(2,1)S(1)}, bf16[1,64,256]{2,1,0:T(8,128)(2,1)S(1)}, u32[]{:S(2)}, u32[]{:S(2)}) collective-permute-start(bf16[1,64,256]{2,1,0:T(8,128)(2,1)S(1)} %get-tuple-element.70), channel_id=1, source_target_pairs={{1,0},{2,1},{3,2},{4,3},{5,4},{6,5},{7,6},{8,7},{9,8},{10,9},{11,1... | collective-permute-start | bytes 98312 | tf_op jit(solution)/shard_map/ppermute | solution.py:10
  122.3 9.4 %collective-permute-start.11 = (bf16[1,64,256]{2,1,0:T(8,128)(2,1)S(1)}, bf16[1,64,256]{2,1,0:T(8,128)(2,1)S(1)}, u32[]{:S(2)}, u32[]{:S(2)}) collective-permute-start(bf16[1,64,256]{2,1,0:T(8,128)(2,1)S(1)} %collective-permute-done.10), channel_id=1, source_target_pairs={{0,64},{16,80},{32,96},{48,112},{64,0},{80,16},{96,32},{112,48},{1... | collective-permute-start | bytes 98312 | tf_op jit(solution)/shard_map/ppermute | solution.py:19
  125.6 7.1 %collective-permute-start.8 = (bf16[1,64,256]{2,1,0:T(8,128)(2,1)S(1)}, bf16[1,64,256]{2,1,0:T(8,128)(2,1)S(1)}, u32[]{:S(2)}, u32[]{:S(2)}) collective-permute-start(bf16[1,64,256]{2,1,0:T(8,128)(2,1)S(1)} %get-tuple-element.71), channel_id=1, source_target_pairs={{0,1},{1,2},{2,3},{3,4},{4,5},{5,6},{6,7},{7,8},{8,9},{9,10},{10,1... | collective-permute-start | bytes 98312 | tf_op jit(solution)/shard_map/ppermute | solution.py:10
  132.8 5.5 collective-permute-start.14
  137.2 6.6 collective-permute-start.13
  152.5 11.1 %collective-permute-start.16 = (bf16[1,64,256]{2,1,0:T(8,128)(2,1)S(1)}, bf16[1,64,256]{2,1,0:T(8,128)(2,1)S(1)}, u32[]{:S(2)}, u32[]{:S(2)}) collective-permute-start(bf16[1,64,256]{2,1,0:T(8,128)(2,1)S(1)} %get-tuple-element.67), channel_id=1, source_target_pairs={{0,16},{16,0},{32,48},{48,32},{64,80},{80,64},{96,112},{112,96},{1... | collective-permute-start | bytes 98312 | tf_op jit(solution)/shard_map/ppermute | solution.py:19
  152.5 14.0 %collective-permute-start.15 = (bf16[1,64,256]{2,1,0:T(8,128)(2,1)S(1)}, bf16[1,64,256]{2,1,0:T(8,128)(2,1)S(1)}, u32[]{:S(2)}, u32[]{:S(2)}) collective-permute-start(bf16[1,64,256]{2,1,0:T(8,128)(2,1)S(1)} %get-tuple-element.67), channel_id=1, source_target_pairs={{0,1},{1,2},{2,3},{3,4},{4,5},{5,6},{6,7},{7,8},{8,9},{9,10},{10,1... | collective-permute-start | bytes 98312 | tf_op jit(solution)/shard_map/ppermute | solution.py:10
  159.3 12.3 %collective-permute-start.19 = (bf16[1,64,256]{2,1,0:T(8,128)(2,1)}, bf16[1,64,256]{2,1,0:T(8,128)(2,1)S(1)}, u32[]{:S(2)}, u32[]{:S(2)}) collective-permute-start(bf16[1,64,256]{2,1,0:T(8,128)(2,1)} %get-tuple-element.66), channel_id=1, source_target_pairs={{1,0},{2,1},{3,2},{4,3},{5,4},{6,5},{7,6},{8,7},{9,8},{10,9},{11,1... | collective-permute-start | bytes 98312 | tf_op jit(solution)/shard_map/ppermute | solution.py:10
  163.6 2.8 collective-permute-start.17
  166.4 4.4 collective-permute-start.18
  171.7 4.8 collective-permute-start.21
  174.4 6.8 collective-permute-start.20
  265.6 16.6 %collective-permute-start.23 = (bf16[3,32,4096]{2,1,0:T(8,128)(2,1)}, bf16[3,32,4096]{2,1,0:T(8,128)(2,1)}, u32[]{:S(2)}, u32[]{:S(2)}) collective-permute-start(bf16[3,32,4096]{2,1,0:T(8,128)(2,1)} %squeeze.110), channel_id=1, source_target_pairs={{1,0},{2,1},{3,2},{4,3},{5,4},{6,5},{7,6},{8,7},{9,8},{10,9},{11,1... | collective-permute-start | bytes 2359304 | tf_op jit(solution)/shard_map/ppermute | solution.py:10
  267.7 15.7 %collective-permute-start.22 = (bf16[3,32,4096]{2,1,0:T(8,128)(2,1)}, bf16[3,32,4096]{2,1,0:T(8,128)(2,1)}, u32[]{:S(2)}, u32[]{:S(2)}) collective-permute-start(bf16[3,32,4096]{2,1,0:T(8,128)(2,1)} %squeeze.109), channel_id=1, source_target_pairs={{0,1},{1,2},{2,3},{3,4},{4,5},{5,6},{6,7},{7,8},{8,9},{9,10},{10,1... | collective-permute-start | bytes 2359304 | tf_op jit(solution)/shard_map/ppermute | solution.py:10
  285.1 26.6 %collective-permute-start.24 = (bf16[3,32,4096]{2,1,0:T(8,128)(2,1)S(1)}, bf16[3,32,4096]{2,1,0:T(8,128)(2,1)S(1)}, u32[]{:S(2)}, u32[]{:S(2)}) collective-permute-start(bf16[3,32,4096]{2,1,0:T(8,128)(2,1)S(1)} %get-tuple-element.30), channel_id=1, source_target_pairs={{0,112},{16,0},{32,16},{48,32},{64,48},{80,64},{96,80},{112,96},{1... | collective-permute-start | bytes 2359304 | tf_op jit(solution)/shard_map/ppermute | solution.py:15
  285.2 39.1 %collective-permute-start.25 = (bf16[3,32,4096]{2,1,0:T(8,128)(2,1)S(1)}, bf16[3,32,4096]{2,1,0:T(8,128)(2,1)S(1)}, u32[]{:S(2)}, u32[]{:S(2)}) collective-permute-start(bf16[3,32,4096]{2,1,0:T(8,128)(2,1)S(1)} %get-tuple-element.31), channel_id=1, source_target_pairs={{0,16},{16,32},{32,48},{48,64},{64,80},{80,96},{96,112},{112,0},{1... | collective-permute-start | bytes 2359304 | tf_op jit(solution)/shard_map/ppermute | solution.py:15
  336.2 350.3 %all-reduce.7.cloned.1.call-start = ((), (), s32[]{:S(2)}) async-start(), calls=%async_computation.1 | async-start | bytes 9699328 | tf_op jit(solution)/shard_map/psum | solution.py:186
  (43 other events, 183.5 us)
Sparse Core Ops, SparseCore 0:
  336.3 134.1 all-reduce.4
  473.5 212.9 all-reduce.6
